TPU v7x, 32 devices: a whole 2x2x4 slice. The times are simulated.
32 devices in a mesh: dp: 16 (over z, y, x), segment: 2 (over core).
Axes of the slice: x: 2, y: 2, z: 4, core: 2. Of those that a mesh axis runs over, the one named last changes fastest.
Arguments:
- latents: bfloat16 [16384, 640], P('dp'), may hold values from -6 to 6
- noise: bfloat16 [16384, 640], P('dp'), may hold values from -6 to 6
- timesteps: int32 [128], P('dp'), may hold values from 100 to 799
- reward_dir: float32 [640], replicated, may hold values from -6 to 6
- gain: float32 [2, 640], P('segment'), may hold values from 0.5 to 1.5
- time_scale: float32 [2, 640], P('segment'), may hold values from -6 to 6
- w_in: bfloat16 [2, 640, 640], P('segment', 'dp'), may hold values from -0.25 to 0.25
- w_out: bfloat16 [2, 640, 640], P('segment', 'dp'), may hold values from -0.25 to 0.25
Outputs:
- weight_grads: float32 [2, 640, 1280], P('segment', 'dp')
All inputs are finite; a program needn't handle non-finite values.
Results may differ from a plain program's by a relative error of at most 0.0004.
Values may be sent and summed in bfloat16 or wider, within the bound.
A program may use at most 64 MiB of HBM per device.

v0:
```python
import functools
import math

import jax
import jax.numpy as jnp
from jax import lax
from jax.experimental import pallas as pl
from jax.experimental.pallas import tpu as pltpu
from jax.sharding import PartitionSpec as P

GROUPS = 32
NSTEPS = 1000
STRIDE = 20
LEAD = 2


EPS = 1e-05


def passed_along(shard, axis, by):
    length = lax.axis_size(axis)
    pairs = [(i, i + by) for i in range(length) if 0 <= i + by < length]
    return lax.ppermute(shard, axis, pairs)


def group_norm(state_f32, group_count):
    channels = state_f32.shape[1]
    per_group = channels // group_count
    col_mean = jnp.mean(state_f32, axis=0)
    group_mean = jnp.repeat(jnp.mean(col_mean.reshape(group_count, per_group), axis=1), per_group)
    centered = state_f32 - group_mean
    sq_mean = jnp.mean(centered * centered, axis=0)
    variance = jnp.repeat(jnp.mean(sq_mean.reshape(group_count, per_group), axis=1), per_group)
    return centered * lax.rsqrt(variance + EPS)


def time_embed(timestep, channels):
    half_width = channels // 2
    frequencies = jnp.exp(
        -math.log(10000.0) * jnp.arange(half_width).astype(jnp.float32) / half_width
    )
    phases = timestep.astype(jnp.float32) * frequencies
    return jnp.concatenate([jnp.sin(phases), jnp.cos(phases)])


def alpha_bar(timestep):
    value = ((timestep.astype(jnp.float32) + 1.0) / NSTEPS + 0.008) / 1.008 * (math.pi / 2.0)
    return jnp.cos(value) ** 2


def contract_rows(left, right):
    return lax.dot_general(
        left, right, (((0,), (0,)), ((), ())), preferred_element_type=jnp.float32
    )


def contract_cols(left, right):
    return lax.dot_general(
        left, right, (((1,), (1,)), ((), ())), preferred_element_type=jnp.float32
    )


def block_forward(hidden, gain_row, temb, first, second):
    state_f32 = hidden.astype(jnp.float32)
    normed = (group_norm(state_f32, GROUPS) * gain_row).astype(jnp.bfloat16)
    preact = jnp.dot(normed, first, preferred_element_type=jnp.float32) + temb
    activation = jax.nn.silu(preact).astype(jnp.bfloat16)
    result = (state_f32 + jnp.dot(activation, second, preferred_element_type=jnp.float32)).astype(
        jnp.bfloat16
    )
    return (result, normed, preact, activation)


def block_backward(hidden, gain_row, preact, cotangent, first, second):
    grad_act = contract_cols(cotangent, second)
    gate_value = jax.nn.sigmoid(preact)
    grad_pre = (grad_act * gate_value * (1.0 + preact * (1.0 - gate_value))).astype(jnp.bfloat16)
    grad_norm = contract_cols(grad_pre, first)
    _, pullback = jax.vjp(lambda values: group_norm(values, GROUPS), hidden.astype(jnp.float32))
    new_cot = (cotangent.astype(jnp.float32) + pullback(grad_norm * gain_row)[0]).astype(
        jnp.bfloat16
    )
    return (new_cot, grad_pre)


def weight_term(normed, grad_pre, activation, cotangent):
    return jnp.concatenate(
        [contract_rows(normed, grad_pre), contract_rows(activation, cotangent)], axis=1
    )


def sample_head(hidden, latent, noise_block, timestep, reward_dir, loss_scale):
    ab_now = alpha_bar(timestep)
    ab_prev = alpha_bar(timestep - STRIDE)
    coef_a = jnp.sqrt(ab_now)
    coef_b = jnp.sqrt(1.0 - ab_now)
    coef_p = jnp.sqrt(ab_prev)
    coef_q = jnp.sqrt(0.75 * (1.0 - ab_prev))
    coef_r = 0.5 * jnp.sqrt(1.0 - ab_prev)
    noise_pred, pullback = jax.vjp(
        lambda values: group_norm(values, GROUPS), hidden.astype(jnp.float32)
    )
    current = latent.astype(jnp.float32)
    previous = (
        coef_p * (current - coef_b * noise_pred) / coef_a
        + coef_q * noise_pred
        + coef_r * noise_block.astype(jnp.float32)
    )
    squashed = jnp.tanh(previous)
    grad_pred = (
        (coef_q - coef_p * coef_b / coef_a) * reward_dir * (1.0 - squashed * squashed) * loss_scale
    )
    return pullback(grad_pred)[0].astype(jnp.bfloat16)


def put_slot(buffer, value, slot_index):
    return lax.dynamic_update_index_in_dim(buffer, value, slot_index, 0)


def body(latents, noise, timesteps, reward_dir, gain, time_scale, w_in, w_out):
    segments = lax.axis_size("segment")
    segment_index = lax.axis_index("segment")
    last_segment = segments - 1
    micro_count = timesteps.shape[0]
    crop_rows = latents.shape[0] // micro_count
    channels = latents.shape[1]
    loss_scale = 1.0 / math.sqrt(lax.axis_size("dp") * latents.shape[0])
    tick_count = micro_count + segments - 1
    whole_in, whole_out = (
        lax.all_gather(w_in, "dp", axis=1, tiled=True),
        lax.all_gather(w_out, "dp", axis=1, tiled=True),
    )
    first = whole_in[0]
    second = whole_out[0]
    gain_row = gain[0]
    latent_blocks = latents.reshape(micro_count, crop_rows, channels)
    noise_blocks = noise.reshape(micro_count, crop_rows, channels)
    embeds = jax.vmap(lambda values: time_embed(values, channels))(timesteps) * time_scale[0]
    blank = jnp.zeros((crop_rows, channels), jnp.bfloat16)
    blank_stack = jnp.zeros((micro_count, crop_rows, channels), jnp.bfloat16)
    stored = ()

    def forward_tick(tick_index, state_carry):
        incoming, inputs, head_cots, kept = state_carry
        micro_index = tick_index - segment_index
        active = (micro_index >= 0) & (micro_index < micro_count)
        slot_index = jnp.clip(micro_index, 0, micro_count - 1)
        fresh_input = latent_blocks[slot_index]
        hidden = jnp.where(segment_index == 0, fresh_input, incoming)

        def forward_compute(buffers):
            inputs, head_cots, kept = buffers
            result, normed, preact, activation = block_forward(
                hidden, gain_row, embeds[slot_index], first, second
            )
            inputs = put_slot(inputs, hidden, slot_index)
            head_cot = lax.cond(
                segment_index == last_segment,
                lambda: sample_head(
                    result,
                    fresh_input,
                    noise_blocks[slot_index],
                    timesteps[slot_index],
                    reward_dir,
                    loss_scale,
                ),
                lambda: blank,
            )
            head_cots = put_slot(head_cots, head_cot, slot_index)
            return (result, inputs, head_cots, kept)

        def forward_skipped(buffers):
            return (blank, buffers[0], buffers[1], buffers[2])

        result, inputs, head_cots, kept = lax.cond(
            active, forward_compute, forward_skipped, (inputs, head_cots, kept)
        )
        incoming = passed_along(result, "segment", 1)
        return (incoming, inputs, head_cots, kept)

    _, inputs, head_cots, kept = lax.fori_loop(
        0, tick_count, forward_tick, (blank, blank_stack, blank_stack, stored)
    )
    grad_start = ()
    records = (blank_stack, blank_stack, blank_stack, blank_stack)

    def backward_tick(tick_index, state_carry):
        incoming, grad_sum, records = state_carry
        micro_index = tick_index - (last_segment - segment_index)
        active = (micro_index >= 0) & (micro_index < micro_count)
        slot_index = jnp.clip(micro_index, 0, micro_count - 1)
        cotangent = jnp.where(segment_index == last_segment, head_cots[slot_index], incoming)

        def backward_compute(buffers):
            grad_sum, records = buffers
            hidden = inputs[slot_index]
            _, normed, preact, activation = block_forward(
                hidden, gain_row, embeds[slot_index], first, second
            )
            new_cot, grad_pre = block_backward(hidden, gain_row, preact, cotangent, first, second)
            records = (
                put_slot(records[0], normed, slot_index),
                put_slot(records[1], grad_pre, slot_index),
                put_slot(records[2], activation, slot_index),
                put_slot(records[3], cotangent, slot_index),
            )
            return (new_cot, grad_sum, records)

        def backward_skipped(buffers):
            return (blank, buffers[0], buffers[1])

        result, grad_sum, records = lax.cond(
            active, backward_compute, backward_skipped, (grad_sum, records)
        )
        incoming = passed_along(result, "segment", -1)
        return (incoming, grad_sum, records)

    _, grad_sum, records = lax.fori_loop(0, tick_count, backward_tick, (blank, grad_start, records))
    flat = [buffer.reshape(micro_count * crop_rows, channels) for buffer in records]
    full_terms = weight_term(flat[0], flat[1], flat[2], flat[3])
    grad_rows = lax.psum_scatter(full_terms, "dp", scatter_dimension=0, tiled=True)
    return grad_rows[None]


def split_rows(values):
    high = values.astype(jnp.bfloat16).astype(jnp.float32)
    rest = values - high
    middle = rest.astype(jnp.bfloat16).astype(jnp.float32)
    low = rest - middle
    return jnp.concatenate([high, middle, low], axis=0).astype(jnp.bfloat16)


class Pair:
    def __init__(self, copies):
        self.copies = copies

    def start(self):
        for copy in self.copies:
            copy.start()

    def wait_recv(self):
        for copy in self.copies:
            copy.wait_recv()

    def wait_send(self):
        for copy in self.copies:
            copy.wait_send()


def step_kernel(
    shape,
    win_ref,
    wout_ref,
    gain_ref,
    time_ref,
    latent_ref,
    noise_ref,
    times_ref,
    reward_ref,
    out_ref,
    embed_ref,
    coef_ref,
    wbuf,
    pbuf,
    weights,
    states,
    noises,
    normed,
    slopes,
    acts,
    cots,
    gradpre,
    means,
    scales,
    sums,
    spread,
    gather_mat,
    scatter_mat,
    grads,
    inbox0,
    inbox1,
    inbox2,
    inbox3,
    result,
    closed,
    send_sem,
    recv_sem,
    local_sem,
):
    dp, depth, shard, channels, images, rows, loss_scale = shape
    me = lax.axis_index("dp")
    core = lax.axis_index("segment")
    other = 1 - core
    col = lax.rem(me, 4)
    z = me // 4
    qx = col + 1 - 2 * lax.rem(col, 2)
    qy = lax.rem(col + 2, 4)
    qd = 3 - col
    x_dev = (z * 4 + qx, core)
    y_dev = (z * 4 + qy, core)
    partner = (me, other)
    z_at = [lax.rem(z + dz, depth) for dz in range(depth)]
    z_from = [lax.rem(z + depth - dz, depth) for dz in range(depth)]
    z_dev = [(z_at[dz] * 4 + col, core) for dz in range(depth)]
    count = [0]
    pending = []

    def reserve(src, dst, device):
        k = count[0]
        count[0] += 1
        copy = pltpu.make_async_remote_copy(
            src_ref=src,
            dst_ref=dst,
            send_sem=send_sem.at[k],
            recv_sem=recv_sem.at[k],
            device_id=device,
            device_id_type=pl.DeviceIdType.MESH,
        )
        return copy

    def remote(src, dst, device):
        copy = reserve(src, dst, device)
        copy.start()
        pending.append(copy)
        return copy

    base = pl.multiple_of(core * (images * rows), images * rows)
    locals_ = [
        pltpu.make_async_copy(source, target, local_sem.at[k])
        for k, (source, target) in enumerate(
            (
                (win_ref.at[0], wbuf.at[core, col, z, 0]),
                (wout_ref.at[0], wbuf.at[core, col, z, 1]),
                (gain_ref, pbuf.at[core, 0]),
                (time_ref, pbuf.at[core, 1]),
                (latent_ref.at[pl.ds(base, images * rows)], states.at[0]),
                (noise_ref.at[pl.ds(base, images * rows)], noises),
            )
        )
    ]
    for copy in locals_:
        copy.start()

    barrier = pltpu.get_barrier_semaphore()
    friends = [x_dev, y_dev, partner] + z_dev[1:]
    for device in friends:
        pl.semaphore_signal(
            barrier, inc=1, device_id=device, device_id_type=pl.DeviceIdType.MESH
        )
    pl.semaphore_wait(barrier, len(friends))

    def own_shard(device):
        return Pair(
            [
                remote(source.at[0], wbuf.at[core, col, z, kind], device)
                for kind, source in enumerate((win_ref, wout_ref))
            ]
        )

    slots = [(way, hop) for hop in range(depth - 1) for way in (1, -1)]

    def holds(way, hop):
        return z >= hop + 1 if way > 0 else z <= depth - 2 - hop

    def goes_on(way):
        return z <= depth - 2 if way > 0 else z >= 1

    def along(way):
        return (lax.rem(z + depth + way, depth) * 4 + col, core)

    own_x, own_y = own_shard(x_dev), own_shard(y_dev)
    line = {}
    for way in (1, -1):
        line[way, 0] = Pair(
            [
                reserve(source.at[0], wbuf.at[core, col, z, kind], along(way))
                for kind, source in enumerate((win_ref, wout_ref))
            ]
        )

        @pl.when(goes_on(way))
        def _(way=way):
            line[way, 0].start()

    to_core = [
        own_shard(partner),
        remote(gain_ref, pbuf.at[core, 0], partner),
        remote(time_ref, pbuf.at[core, 1], partner),
    ]
    ch = lax.broadcasted_iota(jnp.int32, gather_mat.shape, 0)
    gr = lax.broadcasted_iota(jnp.int32, gather_mat.shape, 1) * (channels // GROUPS)
    inside = (ch >= gr) & (ch < gr + channels // GROUPS)
    gather_mat[...] = jnp.where(inside, 1.0, 0.0).astype(jnp.bfloat16)
    ch = lax.broadcasted_iota(jnp.int32, scatter_mat.shape, 1)
    gr = lax.broadcasted_iota(jnp.int32, scatter_mat.shape, 0) * (channels // GROUPS)
    inside = (ch >= gr) & (ch < gr + channels // GROUPS)
    scatter_mat[...] = jnp.where(inside, 1.0, 0.0).astype(jnp.bfloat16)
    sums[...] = jnp.zeros_like(sums)

    def column(stacked):
        line = lax.broadcasted_iota(jnp.int32, stacked.shape, 0)
        values = jnp.zeros(stacked.shape, jnp.float32)
        for i in range(images):
            values = jnp.where(
                line == i, times_ref[core * images + i].astype(jnp.float32), values
            )
        return values

    half_width = channels // 2
    lane = lax.broadcasted_iota(jnp.int32, embed_ref.shape, 1)
    k_index = jnp.where(lane < half_width, lane, lane - half_width).astype(jnp.float32)
    phases = column(embed_ref) * jnp.exp(-math.log(10000.0) * k_index / half_width)
    embed_ref[...] = jnp.where(lane < half_width, jnp.sin(phases), jnp.cos(phases))
    now = column(coef_ref.at[0])
    ab_now, ab_prev = alpha_bar(now), alpha_bar(now - STRIDE)
    coef_a, coef_b = jnp.sqrt(ab_now), jnp.sqrt(1.0 - ab_now)
    coef_p, coef_q = jnp.sqrt(ab_prev), jnp.sqrt(0.75 * (1.0 - ab_prev))
    coef_ref[0] = coef_p / coef_a
    coef_ref[1] = coef_q - coef_p * coef_b / coef_a
    coef_ref[2] = 0.5 * jnp.sqrt(1.0 - ab_prev)

    spread_x, spread_y, diag, core_sends = {}, {}, {}, {}

    def slot_piece(way, hop, q):
        return wbuf.at[core, q, lax.rem(z + depth - way * (hop + 1), depth)]

    for way, hop in slots:
        piece = slot_piece(way, hop, col)
        spread_x[way, hop] = reserve(piece, piece, x_dev)
        spread_y[way, hop] = reserve(piece, piece, y_dev)
        more = [reserve(piece, piece, partner)]
        if hop + 1 < depth - 1:
            line[way, hop + 1] = reserve(piece, piece, along(way))
        core_sends[way, hop] = more

        @pl.when(holds(way, hop))
        def _(way=way, hop=hop, more=more):
            line[way, hop].wait_recv()
            if hop + 1 < depth - 1:

                @pl.when(goes_on(way))
                def _():
                    line[way, hop + 1].start()

            spread_x[way, hop].start()
            spread_y[way, hop].start()
            more[0].start()

    def forward(from_x, from_y, maker):
        return [
            maker(from_x.at[0], from_x.at[0], y_dev),
            maker(from_y.at[1], from_y.at[1], x_dev),
            maker(from_x, from_x, partner),
            maker(from_y, from_y, partner),
        ]

    own_x.wait_recv()
    own_y.wait_recv()
    own_diag = forward(wbuf.at[core, qx, z], wbuf.at[core, qy, z], remote)
    to_core += own_diag[2:]
    for way, hop in slots:
        batch = forward(slot_piece(way, hop, qx), slot_piece(way, hop, qy), reserve)
        diag[way, hop] = batch[:2]
        core_sends[way, hop] += batch[2:]

        @pl.when(holds(way, hop))
        def _(way=way, hop=hop, batch=batch):
            spread_x[way, hop].wait_recv()
            spread_y[way, hop].wait_recv()
            for copy in batch:
                copy.start()

    for copy in own_diag[:2]:
        copy.wait_recv()
    to_core.append(remote(wbuf.at[core, qd, z], wbuf.at[core, qd, z], partner))
    for way, hop in slots:
        piece = slot_piece(way, hop, qd)
        closing_copy = reserve(piece, piece, partner)
        core_sends[way, hop].append(closing_copy)

        @pl.when(holds(way, hop))
        def _(way=way, hop=hop, closing_copy=closing_copy):
            for copy in diag[way, hop]:
                copy.wait_recv()
            closing_copy.start()

    for way, hop in slots:

        @pl.when(holds(way, hop))
        def _(way=way, hop=hop):
            for copy in core_sends[way, hop]:
                copy.wait_recv()

    for copy in locals_:
        copy.wait()
    for copy in to_core:
        copy.wait_recv()

    for section in range(2):
        for kind in range(2):
            for pair in range(dp // 2):
                q, zz = (2 * pair) % 4, pair // 2
                both = jnp.concatenate(
                    [
                        wbuf[section, q, zz, kind].astype(jnp.float32),
                        wbuf[section, q + 1, zz, kind].astype(jnp.float32),
                    ],
                    axis=0,
                )
                weights[section, kind, 2 * pair * shard : 2 * (pair + 1) * shard, :] = (
                    both.astype(jnp.bfloat16)
                )

    def group_means(values):
        parts = jnp.dot(
            split_rows(values), gather_mat[...], preferred_element_type=jnp.float32
        )
        lines = values.shape[0]
        total = parts[:lines] + parts[lines : 2 * lines] + parts[2 * lines :]
        total = total * (1.0 / (rows * (channels // GROUPS)))
        parts = jnp.dot(
            split_rows(total), scatter_mat[...], preferred_element_type=jnp.float32
        )
        return parts[:lines] + parts[lines : 2 * lines] + parts[2 * lines :]

    def statistics(stage):
        def mean_body(i, carry):
            block = states[stage, pl.ds(i * rows, rows), :].astype(jnp.float32)
            sums[pl.ds(i, 1), :] = jnp.sum(block, axis=0, keepdims=True)
            return carry

        lax.fori_loop(0, images, mean_body, 0)
        means[stage] = group_means(sums[...])

        def square_body(i, carry):
            block = states[stage, pl.ds(i * rows, rows), :].astype(jnp.float32)
            centered = block - means[stage, pl.ds(i, 1), :]
            sums[pl.ds(i, 1), :] = jnp.sum(centered * centered, axis=0, keepdims=True)
            return carry

        lax.fori_loop(0, images, square_body, 0)
        scales[stage] = lax.rsqrt(group_means(sums[...]) + EPS)

    def unit(stage, i):
        block = states[stage, pl.ds(i * rows, rows), :].astype(jnp.float32)
        return (block - means[stage, pl.ds(i, 1), :]) * scales[stage, pl.ds(i, 1), :]

    joint = 2 if images % 2 == 0 else 1
    for section in range(2):
        statistics(section)
        gain_row = pbuf[section, 0]
        time_row = pbuf[section, 1]

        def forward_body(g, carry):
            for j in range(joint):
                i = g * joint + j
                where = pl.ds(pl.multiple_of(i * rows, rows), rows)
                normed[section, where, :] = (unit(section, i) * gain_row).astype(jnp.bfloat16)
            span = pl.ds(pl.multiple_of(g * joint * rows, rows), joint * rows)
            product = jnp.dot(
                normed[section, span, :],
                weights[section, 0],
                preferred_element_type=jnp.float32,
            )
            for j in range(joint):
                i = g * joint + j
                where = pl.ds(pl.multiple_of(i * rows, rows), rows)
                preact = product[j * rows : (j + 1) * rows] + time_row * embed_ref[pl.ds(i, 1), :]
                gate = jax.nn.sigmoid(preact)
                acts[section, where, :] = (preact * gate).astype(jnp.bfloat16)
                slopes[section, where, :] = gate * (1.0 + preact * (1.0 - gate))
            product = jnp.dot(
                acts[section, span, :],
                weights[section, 1],
                preferred_element_type=jnp.float32,
            )
            states[section + 1, span, :] = (
                states[section, span, :].astype(jnp.float32) + product
            ).astype(jnp.bfloat16)
            return carry

        lax.fori_loop(0, images // joint, forward_body, 0)

    statistics(2)

    def head_body(i, carry):
        where = pl.ds(pl.multiple_of(i * rows, rows), rows)
        pred = unit(2, i)
        current = states[0, where, :].astype(jnp.float32)
        fresh = noises[where, :].astype(jnp.float32)
        keep, pull, stir = (coef_ref[j, pl.ds(i, 1), 0:1] for j in range(3))
        squashed = jnp.tanh(keep * current + pull * pred + stir * fresh)
        grad = (1.0 - squashed * squashed) * (reward_ref[...][None] * (pull * loss_scale))
        spread[where, :] = grad
        sums[pl.ds(i, 1), :] = jnp.sum(grad, axis=0, keepdims=True)
        sums[pl.ds(images + i, 1), :] = jnp.sum(grad * pred, axis=0, keepdims=True)
        return carry

    lax.fori_loop(0, images, head_body, 0)

    def pull_back(stage, incoming):
        means_two = group_means(sums[...])
        sums[...] = means_two

        def body(i, carry):
            where = pl.ds(pl.multiple_of(i * rows, rows), rows)
            pulled = scales[stage, pl.ds(i, 1), :] * (
                spread[where, :]
                - sums[pl.ds(i, 1), :]
                - unit(stage, i) * sums[pl.ds(images + i, 1), :]
            )
            if incoming is not None:
                pulled = cots[incoming, where, :].astype(jnp.float32) + pulled
            cots[stage - 1, where, :] = pulled.astype(jnp.bfloat16)
            return carry

        lax.fori_loop(0, images, body, 0)

    pull_back(2, None)

    qa = qx + core * (qy - qx)
    qb = qy + core * (qx - qy)
    a_dev, b_dev = (z * 4 + qa, core), (z * 4 + qb, core)
    own_order, their_order = (qd, qa, qb, col), (qd, qb, qa, col)
    chunks = list(range(depth - 1, 0, -1)) + [0]
    pieces = [(section, dz) for section in (1, 0) for dz in chunks]
    swaps, first, final, last = {}, {}, {}, {}

    def mine(section, q, dz):
        return grads.at[section, core, q, z_at[dz]]

    def add(target, source):
        target[...] = target[...] + source[...]

    def swap(section):
        for dz in chunks:
            for step in range(4):
                q = their_order[step]
                swaps[section, dz, step] = remote(
                    grads.at[section, other, q, z_at[dz]],
                    inbox0.at[section, q, z_at[dz]],
                    partner,
                )

    def summed(section, dz, step):
        q = own_order[step]
        swaps[section, dz, step].wait_recv()
        target = mine(section, q, dz)
        add(target, inbox0.at[section, q, z_at[dz]])
        return target

    def stage_one(section, dz):
        for step in range(2):
            first[section, dz, step] = remote(
                summed(section, dz, step), inbox1.at[section, step, z_at[dz]], a_dev
            )

    def stage_two(section, dz):
        total = summed(section, dz, 2)
        first[section, dz, 0].wait_recv()
        add(total, inbox1.at[section, 0, z_at[dz]])
        final[section, dz] = remote(total, inbox2.at[section, z_at[dz]], b_dev)

    def stage_three(section, dz):
        total = summed(section, dz, 3)
        first[section, dz, 1].wait_recv()
        add(total, inbox1.at[section, 1, z_at[dz]])
        final[section, dz].wait_recv()
        add(total, inbox2.at[section, z_at[dz]])
        if dz > 0:
            last[section, dz] = remote(total, inbox3.at[section, dz], z_dev[dz])

    def turn_of(turn):
        for lag, stage in ((0, stage_one), (LEAD, stage_two), (LEAD + 1, stage_three)):
            if 0 <= turn - lag < len(pieces):
                stage(*pieces[turn - lag])

    def weight_grad(section, kind):
        if kind == 0:
            term = contract_rows(normed[section], gradpre[section])
        else:
            term = contract_rows(acts[section], cots[section])
        for owner in range(dp):
            grads[section, kind, owner % 4, owner // 4] = term[
                owner * shard : (owner + 1) * shard
            ]

    def grad_preact(section):
        def body(g, carry):
            span = pl.ds(pl.multiple_of(g * joint * rows, rows), joint * rows)
            product = contract_cols(cots[section, span, :], weights[section, 1])
            gradpre[section, span, :] = (product * slopes[section, span, :]).astype(jnp.bfloat16)
            return carry

        lax.fori_loop(0, images // joint, body, 0)

    def grad_normed(section):
        gain_row = pbuf[section, 0]

        def body(g, carry):
            span = pl.ds(pl.multiple_of(g * joint * rows, rows), joint * rows)
            product = contract_cols(gradpre[section, span, :], weights[section, 0])
            for j in range(joint):
                i = g * joint + j
                where = pl.ds(pl.multiple_of(i * rows, rows), rows)
                grad = product[j * rows : (j + 1) * rows] * gain_row
                spread[where, :] = grad
                sums[pl.ds(i, 1), :] = jnp.sum(grad, axis=0, keepdims=True)
                sums[pl.ds(images + i, 1), :] = jnp.sum(
                    grad * unit(section, i), axis=0, keepdims=True
                )
            return carry

        lax.fori_loop(0, images // joint, body, 0)

    grad_preact(1)
    weight_grad(1, 1)
    weight_grad(1, 0)
    swap(1)
    grad_normed(1)
    turn_of(0)
    pull_back(1, 1)
    turn_of(1)
    grad_preact(0)
    turn_of(2)
    weight_grad(0, 1)
    turn_of(3)
    weight_grad(0, 0)
    swap(0)
    for turn in range(4, len(pieces) + LEAD + 1):
        turn_of(turn)
    for section in (1, 0):
        total = mine(section, col, 0)[...]
        for dz in chunks[:-1]:
            last[section, dz].wait_recv()
            total = total + inbox3[section, dz]
        result[section] = total
    closing = remote(result.at[other], closed, partner)
    closing.wait_recv()
    ours, theirs = result[core], closed[...]
    out_ref[0, :, :channels] = jnp.where(core == 0, ours, theirs)
    out_ref[0, :, channels:] = jnp.where(core == 0, theirs, ours)
    for copy in pending:
        copy.wait_send()
    for way in (1, -1):

        @pl.when(goes_on(way))
        def _(way=way):
            line[way, 0].wait_send()

    for way, hop in slots:

        @pl.when(holds(way, hop))
        def _(way=way, hop=hop):
            sent = [spread_x[way, hop], spread_y[way, hop]] + diag[way, hop]
            for copy in sent + core_sends[way, hop]:
                copy.wait_send()
            if hop + 1 < depth - 1:

                @pl.when(goes_on(way))
                def _():
                    line[way, hop + 1].wait_send()


def fused_body(latents, noise, timesteps, reward_dir, gain, time_scale, w_in, w_out):
    dp = lax.axis_size("dp")
    depth = dp // 4
    micro_count = timesteps.shape[0]
    images = micro_count // 2
    rows = latents.shape[0] // micro_count
    channels = latents.shape[1]
    shard = w_in.shape[1]
    loss_scale = 1.0 / math.sqrt(dp * latents.shape[0])
    shape = (dp, depth, shard, channels, images, rows, loss_scale)
    total_rows = images * rows
    bf16, f32 = jnp.bfloat16, jnp.float32
    lines = -(-2 * images // 8) * 8
    square = (shard, channels)
    copies = 64 * depth
    vmem = pl.BlockSpec(memory_space=pltpu.VMEM)
    grad_rows = pl.pallas_call(
        functools.partial(step_kernel, shape),
        out_shape=jax.ShapeDtypeStruct((1, shard, 2 * channels), f32),
        in_specs=[vmem] * 4 + [pl.BlockSpec(memory_space=pl.ANY)] * 2
        + [pl.BlockSpec(memory_space=pltpu.SMEM), vmem],
        out_specs=vmem,
        scratch_shapes=[
            pltpu.VMEM((-(-images // 8) * 8, channels), f32),
            pltpu.VMEM((3, -(-images // 8) * 8, 128), f32),
            pltpu.VMEM((2, 4, depth, 2) + square, bf16),
            pltpu.VMEM((2, 2, 1, channels), f32),
            pltpu.VMEM((2, 2, channels, channels), bf16),
            pltpu.VMEM((3, total_rows, channels), bf16),
            pltpu.VMEM((total_rows, channels), bf16),
            pltpu.VMEM((2, total_rows, channels), bf16),
            pltpu.VMEM((2, total_rows, channels), f32),
            pltpu.VMEM((2, total_rows, channels), bf16),
            pltpu.VMEM((2, total_rows, channels), bf16),
            pltpu.VMEM((2, total_rows, channels), bf16),
            pltpu.VMEM((3, lines, channels), f32),
            pltpu.VMEM((3, lines, channels), f32),
            pltpu.VMEM((lines, channels), f32),
            pltpu.VMEM((total_rows, channels), f32),
            pltpu.VMEM((channels, 128), bf16),
            pltpu.VMEM((128, channels), bf16),
            pltpu.VMEM((2, 2, 4, depth) + square, f32),
            pltpu.VMEM((2, 4, depth) + square, f32),
            pltpu.VMEM((2, 2, depth) + square, f32),
            pltpu.VMEM((2, depth) + square, f32),
            pltpu.VMEM((2, depth) + square, f32),
            pltpu.VMEM((2,) + square, f32),
            pltpu.VMEM(square, f32),
            pltpu.SemaphoreType.DMA((copies,)),
            pltpu.SemaphoreType.DMA((copies,)),
            pltpu.SemaphoreType.DMA((6,)),
        ],
        compiler_params=pltpu.CompilerParams(
            collective_id=0, has_side_effects=True, vmem_limit_bytes=60 * 1024 * 1024
        ),
    )(w_in, w_out, gain, time_scale, latents, noise, timesteps, reward_dir)
    return grad_rows


def fits(mesh):
    return mesh.shape["segment"] == 2 and mesh.shape["dp"] % 4 == 0 and mesh.shape["dp"] >= 16


def solution(mesh):
    placed = (
        P("dp", None),
        P("dp", None),
        P("dp"),
        P(),
        P("segment", None),
        P("segment", None),
        P("segment", "dp", None),
        P("segment", "dp", None),
    )
    return jax.shard_map(
        fused_body if fits(mesh) else body, mesh=mesh, in_specs=placed, out_specs=P("segment", "dp", None), check_vma=False
    )
```

profile of v0, /device:TPU:0, one launch (start us, length us, event | category | flops | bytes accessed | tf_op | source)
XLA Modules:
  0.0 78.6 jit_solution(3539655478938852411)
XLA Ops:
  0.0 77.0 %shard_map.82 = f32[1,40,1280]{2,1,0:T(8,128)} custom-call(bf16[1,40,640]{2,1,0:T(8,128)(2,1)} %win_ref.1, bf16[1,40,640]{2,1,0:T(8,128)(2,1)} %wout_ref.1, f32[1,640]{1,0:T(1,128)} %gain_ref.1, f32[1,640]{1,0:T(1,128)} %time_ref.1, bf16[1024,640]{1,0:T(8,128)(2,1)} %latent_ref.1, bf16[1024,640]{1,0:T(8,128)(2,1)} %noise_ref.1, s32[8]{0:T(128)} %times_ref.1, ...), custom_call_target="tpu_custom_call" | custom-call | tf_op jit(solution)/shard_map/pallas_call | solution.py:781
  77.0 1.6 %copy.10 = f32[1,40,1280]{2,1,0:T(8,128)} copy(f32[1,40,1280]{2,1,0:T(8,128)} %shard_map.82) | data formatting | bytes 409600
where the time goes:
time: 78.8 us; the launch traced here: 78.6 us
  Pallas kernels  77 us (98%)
  local copies, waits for them, and re-layouts  1.62 us (2%)
    pallas_call x1, Pallas kernels, fused_body(): pl.pallas_call(functools.partial(step_kernel, shape), out_shape=jax.Shape...  77 us
    unnamed x1, local copies, waits for them, and re-layouts  1.62 us

commit v1 on v0

--- a/solution.py
+++ b/solution.py
@@ -11,7 +11,8 @@
 GROUPS = 32
 NSTEPS = 1000
 STRIDE = 20
-LEAD = 2
+LIMIT = 32760.0
+TINY = 1e-30
 
 
 EPS = 1e-05
@@ -230,21 +231,14 @@
     return jnp.concatenate([high, middle, low], axis=0).astype(jnp.bfloat16)
 
 
-class Pair:
-    def __init__(self, copies):
-        self.copies = copies
-
-    def start(self):
-        for copy in self.copies:
-            copy.start()
-
-    def wait_recv(self):
-        for copy in self.copies:
-            copy.wait_recv()
-
-    def wait_send(self):
-        for copy in self.copies:
-            copy.wait_send()
+def encode(block, code_ref, size_ref):
+    top = jnp.maximum(jnp.max(jnp.abs(block), axis=0, keepdims=True), TINY)
+    size_ref[...] = top * (1.0 / LIMIT)
+    code_ref[...] = jnp.round(block * (LIMIT / top)).astype(jnp.int32).astype(jnp.int16)
+
+
+def decode(code_ref, size_ref):
+    return code_ref[...].astype(jnp.int32).astype(jnp.float32) * size_ref[...]
 
 
 def step_kernel(
@@ -277,17 +271,24 @@
     gather_mat,
     scatter_mat,
     grads,
-    inbox0,
-    inbox1,
-    inbox2,
-    inbox3,
-    result,
-    closed,
+    code_a,
+    code_b,
+    code_z,
+    size_a,
+    size_b,
+    size_z,
+    in_a,
+    in_b,
+    in_z,
+    insize_a,
+    insize_b,
+    insize_z,
     send_sem,
     recv_sem,
     local_sem,
 ):
     dp, depth, shard, channels, images, rows, loss_scale = shape
+    total_rows = images * rows
     me = lax.axis_index("dp")
     core = lax.axis_index("segment")
     other = 1 - core
@@ -299,11 +300,23 @@
     x_dev = (z * 4 + qx, core)
     y_dev = (z * 4 + qy, core)
     partner = (me, other)
-    z_at = [lax.rem(z + dz, depth) for dz in range(depth)]
-    z_from = [lax.rem(z + depth - dz, depth) for dz in range(depth)]
-    z_dev = [(z_at[dz] * 4 + col, core) for dz in range(depth)]
+
+    def flipped(j):
+        place = z
+        bit = 1
+        while bit < depth:
+            if j & bit:
+                place = place + bit * (1 - 2 * lax.rem(z // bit, 2))
+            bit *= 2
+        return place
+
+    zj = [flipped(j) for j in range(depth)]
+    z_dev = [(zj[j] * 4 + col, core) for j in range(depth)]
+    far = list(range(1, depth))
+    early = list(range(depth // 2))
+    late = list(range(depth // 2, depth))
     count = [0]
-    pending = []
+    sent = []
 
     def reserve(src, dst, device):
         k = count[0]
@@ -316,25 +329,20 @@
             device_id=device,
             device_id_type=pl.DeviceIdType.MESH,
         )
+        sent.append(copy)
         return copy
 
-    def remote(src, dst, device):
-        copy = reserve(src, dst, device)
-        copy.start()
-        pending.append(copy)
-        return copy
-
-    base = pl.multiple_of(core * (images * rows), images * rows)
+    base = pl.multiple_of(core * total_rows, total_rows)
     locals_ = [
         pltpu.make_async_copy(source, target, local_sem.at[k])
         for k, (source, target) in enumerate(
             (
-                (win_ref.at[0], wbuf.at[core, col, z, 0]),
-                (wout_ref.at[0], wbuf.at[core, col, z, 1]),
+                (win_ref.at[0], wbuf.at[core, 0, col, z]),
+                (wout_ref.at[0], wbuf.at[core, 1, col, z]),
                 (gain_ref, pbuf.at[core, 0]),
                 (time_ref, pbuf.at[core, 1]),
-                (latent_ref.at[pl.ds(base, images * rows)], states.at[0]),
-                (noise_ref.at[pl.ds(base, images * rows)], noises),
+                (latent_ref.at[pl.ds(base, total_rows)], states.at[0]),
+                (noise_ref.at[pl.ds(base, total_rows)], noises),
             )
         )
     ]
@@ -347,46 +355,6 @@
         pl.semaphore_signal(
             barrier, inc=1, device_id=device, device_id_type=pl.DeviceIdType.MESH
         )
-    pl.semaphore_wait(barrier, len(friends))
-
-    def own_shard(device):
-        return Pair(
-            [
-                remote(source.at[0], wbuf.at[core, col, z, kind], device)
-                for kind, source in enumerate((win_ref, wout_ref))
-            ]
-        )
-
-    slots = [(way, hop) for hop in range(depth - 1) for way in (1, -1)]
-
-    def holds(way, hop):
-        return z >= hop + 1 if way > 0 else z <= depth - 2 - hop
-
-    def goes_on(way):
-        return z <= depth - 2 if way > 0 else z >= 1
-
-    def along(way):
-        return (lax.rem(z + depth + way, depth) * 4 + col, core)
-
-    own_x, own_y = own_shard(x_dev), own_shard(y_dev)
-    line = {}
-    for way in (1, -1):
-        line[way, 0] = Pair(
-            [
-                reserve(source.at[0], wbuf.at[core, col, z, kind], along(way))
-                for kind, source in enumerate((win_ref, wout_ref))
-            ]
-        )
-
-        @pl.when(goes_on(way))
-        def _(way=way):
-            line[way, 0].start()
-
-    to_core = [
-        own_shard(partner),
-        remote(gain_ref, pbuf.at[core, 0], partner),
-        remote(time_ref, pbuf.at[core, 1], partner),
-    ]
     ch = lax.broadcasted_iota(jnp.int32, gather_mat.shape, 0)
     gr = lax.broadcasted_iota(jnp.int32, gather_mat.shape, 1) * (channels // GROUPS)
     inside = (ch >= gr) & (ch < gr + channels // GROUPS)
@@ -396,6 +364,96 @@
     inside = (ch >= gr) & (ch < gr + channels // GROUPS)
     scatter_mat[...] = jnp.where(inside, 1.0, 0.0).astype(jnp.bfloat16)
     sums[...] = jnp.zeros_like(sums)
+    for copy in locals_[:4]:
+        copy.wait()
+    pl.semaphore_wait(barrier, len(friends))
+
+    def piece(section, q, j):
+        return wbuf.at[section, core, q, zj[j]]
+
+    swap = [
+        reserve(wbuf.at[core, kind, col, z], wbuf.at[core, kind, col, z], partner)
+        for kind in (0, 1)
+    ]
+    tunes = [
+        reserve(gain_ref, pbuf.at[core, 0], partner),
+        reserve(time_ref, pbuf.at[core, 1], partner),
+    ]
+    to_x, to_y, to_z, to_core, to_diag, blocks = {}, {}, {}, {}, {}, {}
+    for section in range(2):
+        for j in range(depth):
+            here = piece(section, col, j)
+            to_x[section, j] = reserve(here, here, x_dev)
+            to_y[section, j] = reserve(here, here, y_dev)
+            if j > 0:
+                to_core[section, j] = reserve(here, here, partner)
+                own = piece(section, col, 0)
+                to_z[section, j] = reserve(own, own, z_dev[j])
+            q, device = (qx, y_dev) if j in early else (qy, x_dev)
+            passed = piece(section, q, j)
+            to_diag[section, j] = reserve(passed, passed, device)
+        for q, name in ((qx, "x"), (qy, "y"), (qd, "d")):
+            whole = wbuf.at[section, core, q]
+            blocks[section, name] = reserve(whole, whole, partner)
+
+    def send_own(section):
+        to_x[section, 0].start()
+        to_y[section, 0].start()
+        for j in far:
+            to_z[section, j].start()
+
+    def take_swap():
+        for copy in swap:
+            copy.wait_recv()
+
+    for copy in swap:
+        copy.start()
+    for mine in range(2):
+
+        @pl.when(core == mine)
+        def _(mine=mine):
+            send_own(mine)
+
+    take_swap()
+    for mine in range(2):
+
+        @pl.when(core == mine)
+        def _(mine=mine):
+            send_own(1 - mine)
+
+    for copy in tunes:
+        copy.start()
+
+    def pass_line(section, steps):
+        for j in steps:
+            to_z[section, j].wait_recv()
+            to_x[section, j].start()
+            to_y[section, j].start()
+            to_core[section, j].start()
+
+    def pass_diag(section, steps):
+        for j in steps:
+            (to_x if j in early else to_y)[section, j].wait_recv()
+            to_diag[section, j].start()
+
+    def pass_sides(section):
+        for j in late:
+            to_x[section, j].wait_recv()
+        blocks[section, "x"].start()
+        for j in early:
+            to_y[section, j].wait_recv()
+        blocks[section, "y"].start()
+
+    def pass_corner(section):
+        for j in range(depth):
+            to_diag[section, j].wait_recv()
+        blocks[section, "d"].start()
+
+    def arrived(section):
+        for j in far:
+            to_core[section, j].wait_recv()
+        for name in ("x", "y", "d"):
+            blocks[section, name].wait_recv()
 
     def column(stacked):
         line = lax.broadcasted_iota(jnp.int32, stacked.shape, 0)
@@ -419,98 +477,6 @@
     coef_ref[1] = coef_q - coef_p * coef_b / coef_a
     coef_ref[2] = 0.5 * jnp.sqrt(1.0 - ab_prev)
 
-    spread_x, spread_y, diag, core_sends = {}, {}, {}, {}
-
-    def slot_piece(way, hop, q):
-        return wbuf.at[core, q, lax.rem(z + depth - way * (hop + 1), depth)]
-
-    for way, hop in slots:
-        piece = slot_piece(way, hop, col)
-        spread_x[way, hop] = reserve(piece, piece, x_dev)
-        spread_y[way, hop] = reserve(piece, piece, y_dev)
-        more = [reserve(piece, piece, partner)]
-        if hop + 1 < depth - 1:
-            line[way, hop + 1] = reserve(piece, piece, along(way))
-        core_sends[way, hop] = more
-
-        @pl.when(holds(way, hop))
-        def _(way=way, hop=hop, more=more):
-            line[way, hop].wait_recv()
-            if hop + 1 < depth - 1:
-
-                @pl.when(goes_on(way))
-                def _():
-                    line[way, hop + 1].start()
-
-            spread_x[way, hop].start()
-            spread_y[way, hop].start()
-            more[0].start()
-
-    def forward(from_x, from_y, maker):
-        return [
-            maker(from_x.at[0], from_x.at[0], y_dev),
-            maker(from_y.at[1], from_y.at[1], x_dev),
-            maker(from_x, from_x, partner),
-            maker(from_y, from_y, partner),
-        ]
-
-    own_x.wait_recv()
-    own_y.wait_recv()
-    own_diag = forward(wbuf.at[core, qx, z], wbuf.at[core, qy, z], remote)
-    to_core += own_diag[2:]
-    for way, hop in slots:
-        batch = forward(slot_piece(way, hop, qx), slot_piece(way, hop, qy), reserve)
-        diag[way, hop] = batch[:2]
-        core_sends[way, hop] += batch[2:]
-
-        @pl.when(holds(way, hop))
-        def _(way=way, hop=hop, batch=batch):
-            spread_x[way, hop].wait_recv()
-            spread_y[way, hop].wait_recv()
-            for copy in batch:
-                copy.start()
-
-    for copy in own_diag[:2]:
-        copy.wait_recv()
-    to_core.append(remote(wbuf.at[core, qd, z], wbuf.at[core, qd, z], partner))
-    for way, hop in slots:
-        piece = slot_piece(way, hop, qd)
-        closing_copy = reserve(piece, piece, partner)
-        core_sends[way, hop].append(closing_copy)
-
-        @pl.when(holds(way, hop))
-        def _(way=way, hop=hop, closing_copy=closing_copy):
-            for copy in diag[way, hop]:
-                copy.wait_recv()
-            closing_copy.start()
-
-    for way, hop in slots:
-
-        @pl.when(holds(way, hop))
-        def _(way=way, hop=hop):
-            for copy in core_sends[way, hop]:
-                copy.wait_recv()
-
-    for copy in locals_:
-        copy.wait()
-    for copy in to_core:
-        copy.wait_recv()
-
-    for section in range(2):
-        for kind in range(2):
-            for pair in range(dp // 2):
-                q, zz = (2 * pair) % 4, pair // 2
-                both = jnp.concatenate(
-                    [
-                        wbuf[section, q, zz, kind].astype(jnp.float32),
-                        wbuf[section, q + 1, zz, kind].astype(jnp.float32),
-                    ],
-                    axis=0,
-                )
-                weights[section, kind, 2 * pair * shard : 2 * (pair + 1) * shard, :] = (
-                    both.astype(jnp.bfloat16)
-                )
-
     def group_means(values):
         parts = jnp.dot(
             split_rows(values), gather_mat[...], preferred_element_type=jnp.float32
@@ -545,20 +511,42 @@
         block = states[stage, pl.ds(i * rows, rows), :].astype(jnp.float32)
         return (block - means[stage, pl.ds(i, 1), :]) * scales[stage, pl.ds(i, 1), :]
 
-    joint = 2 if images % 2 == 0 else 1
-    for section in range(2):
+    def normalize(section):
         statistics(section)
         gain_row = pbuf[section, 0]
+
+        def norm_body(i, carry):
+            where = pl.ds(pl.multiple_of(i * rows, rows), rows)
+            normed[section, 0, where, :] = (unit(section, i) * gain_row).astype(jnp.bfloat16)
+            return carry
+
+        lax.fori_loop(0, images, norm_body, 0)
+
+    def lay_out(section):
+        for kind in range(2):
+            for pair in range(dp // 2):
+                q, zz = (2 * pair) % 4, pair // 2
+                both = jnp.concatenate(
+                    [
+                        wbuf[section, kind, q, zz].astype(jnp.float32),
+                        wbuf[section, kind, q + 1, zz].astype(jnp.float32),
+                    ],
+                    axis=0,
+                )
+                weights[section, kind, 2 * pair * shard : 2 * (pair + 1) * shard, :] = (
+                    both.astype(jnp.bfloat16)
+                )
+
+    joint = 2 if images % 2 == 0 else 1
+    groups = images // joint
+
+    def forward(section, start, stop):
         time_row = pbuf[section, 1]
 
         def forward_body(g, carry):
-            for j in range(joint):
-                i = g * joint + j
-                where = pl.ds(pl.multiple_of(i * rows, rows), rows)
-                normed[section, where, :] = (unit(section, i) * gain_row).astype(jnp.bfloat16)
             span = pl.ds(pl.multiple_of(g * joint * rows, rows), joint * rows)
             product = jnp.dot(
-                normed[section, span, :],
+                normed[section, 0, span, :],
                 weights[section, 0],
                 preferred_element_type=jnp.float32,
             )
@@ -567,10 +555,10 @@
                 where = pl.ds(pl.multiple_of(i * rows, rows), rows)
                 preact = product[j * rows : (j + 1) * rows] + time_row * embed_ref[pl.ds(i, 1), :]
                 gate = jax.nn.sigmoid(preact)
-                acts[section, where, :] = (preact * gate).astype(jnp.bfloat16)
+                acts[section, 0, where, :] = (preact * gate).astype(jnp.bfloat16)
                 slopes[section, where, :] = gate * (1.0 + preact * (1.0 - gate))
             product = jnp.dot(
-                acts[section, span, :],
+                acts[section, 0, span, :],
                 weights[section, 1],
                 preferred_element_type=jnp.float32,
             )
@@ -579,7 +567,41 @@
             ).astype(jnp.bfloat16)
             return carry
 
-        lax.fori_loop(0, images // joint, forward_body, 0)
+        lax.fori_loop(start, stop, forward_body, 0)
+
+    pass_line(0, far[:1])
+    for copy in tunes:
+        copy.wait_recv()
+    for copy in locals_[4:]:
+        copy.wait()
+    pass_diag(0, early[:1])
+    pass_line(0, far[1:])
+    pass_diag(0, early[1:])
+    pass_line(1, far[:1])
+    normalize(0)
+    pass_diag(0, late)
+    pass_line(1, far[1:])
+    pass_sides(0)
+    pass_corner(0)
+    pass_diag(1, early)
+    arrived(0)
+    lay_out(0)
+    forward(0, 0, groups // 2)
+    pass_diag(1, late)
+    pass_sides(1)
+    forward(0, groups // 2, groups)
+    pass_corner(1)
+    normalize(1)
+    arrived(1)
+    lay_out(1)
+    forward(1, 0, groups)
+
+    share = {
+        name: reserve(ref.at[other, 0], ref.at[other, 1], partner)
+        for name, ref in (("normed", normed), ("acts", acts), ("cots", cots), ("gradpre", gradpre))
+    }
+    share["acts"].start()
+    share["normed"].start()
 
     statistics(2)
 
@@ -610,96 +632,110 @@
                 - unit(stage, i) * sums[pl.ds(images + i, 1), :]
             )
             if incoming is not None:
-                pulled = cots[incoming, where, :].astype(jnp.float32) + pulled
-            cots[stage - 1, where, :] = pulled.astype(jnp.bfloat16)
+                pulled = cots[incoming, 0, where, :].astype(jnp.float32) + pulled
+            cots[stage - 1, 0, where, :] = pulled.astype(jnp.bfloat16)
             return carry
 
         lax.fori_loop(0, images, body, 0)
 
     pull_back(2, None)
 
-    qa = qx + core * (qy - qx)
-    qb = qy + core * (qx - qy)
-    a_dev, b_dev = (z * 4 + qa, core), (z * 4 + qb, core)
-    own_order, their_order = (qd, qa, qb, col), (qd, qb, qa, col)
-    chunks = list(range(depth - 1, 0, -1)) + [0]
-    pieces = [(section, dz) for section in (1, 0) for dz in chunks]
-    swaps, first, final, last = {}, {}, {}, {}
-
-    def mine(section, q, dz):
-        return grads.at[section, core, q, z_at[dz]]
-
-    def add(target, source):
-        target[...] = target[...] + source[...]
-
-    def swap(section):
-        for dz in chunks:
-            for step in range(4):
-                q = their_order[step]
-                swaps[section, dz, step] = remote(
-                    grads.at[section, other, q, z_at[dz]],
-                    inbox0.at[section, q, z_at[dz]],
-                    partner,
+    halves = (late[::-1], early[::-1])
+    sides = (qx, qy)
+    side_devs = (x_dev, y_dev)
+    hop_a, hop_a_size, hop_b, hop_b_size, hop_z, hop_z_size = {}, {}, {}, {}, {}, {}
+    for kind in (1, 0):
+        for h in range(2):
+            for step in range(2):
+                hop_a[kind, h, step] = reserve(
+                    code_a.at[kind, h, step], in_a.at[kind, h, step], side_devs[h]
                 )
-
-    def summed(section, dz, step):
-        q = own_order[step]
-        swaps[section, dz, step].wait_recv()
-        target = mine(section, q, dz)
-        add(target, inbox0.at[section, q, z_at[dz]])
-        return target
-
-    def stage_one(section, dz):
-        for step in range(2):
-            first[section, dz, step] = remote(
-                summed(section, dz, step), inbox1.at[section, step, z_at[dz]], a_dev
-            )
-
-    def stage_two(section, dz):
-        total = summed(section, dz, 2)
-        first[section, dz, 0].wait_recv()
-        add(total, inbox1.at[section, 0, z_at[dz]])
-        final[section, dz] = remote(total, inbox2.at[section, z_at[dz]], b_dev)
-
-    def stage_three(section, dz):
-        total = summed(section, dz, 3)
-        first[section, dz, 1].wait_recv()
-        add(total, inbox1.at[section, 1, z_at[dz]])
-        final[section, dz].wait_recv()
-        add(total, inbox2.at[section, z_at[dz]])
-        if dz > 0:
-            last[section, dz] = remote(total, inbox3.at[section, dz], z_dev[dz])
-
-    def turn_of(turn):
-        for lag, stage in ((0, stage_one), (LEAD, stage_two), (LEAD + 1, stage_three)):
-            if 0 <= turn - lag < len(pieces):
-                stage(*pieces[turn - lag])
+            hop_a_size[kind, h] = reserve(
+                size_a.at[kind, h], insize_a.at[kind, h], side_devs[h]
+            )
+            hop_b[kind, h] = reserve(code_b.at[kind, h], in_b.at[kind, h], side_devs[1 - h])
+            hop_b_size[kind, h] = reserve(
+                size_b.at[kind, h], insize_b.at[kind, h], side_devs[1 - h]
+            )
+        for j in far:
+            hop_z[kind, j] = reserve(code_z.at[kind, j - 1], in_z.at[kind, j - 1], z_dev[j])
+            hop_z_size[kind, j] = reserve(
+                size_z.at[kind, j - 1], insize_z.at[kind, j - 1], z_dev[j]
+            )
+
+    def strip(kind, q, h):
+        return jnp.concatenate([grads[kind, q, zj[j]] for j in halves[h]], axis=0)
+
+    def stage_one(kind):
+        for h in range(2):
+            for step, q in enumerate((qd, sides[h])):
+                encode(strip(kind, q, h), code_a.at[kind, h, step], size_a.at[kind, h, step])
+            hop_a_size[kind, h].start()
+            for step in range(2):
+                hop_a[kind, h, step].start()
+
+    def stage_two(kind):
+        for h in range(2):
+            hop_a_size[kind, h].wait_recv()
+            hop_a[kind, h, 0].wait_recv()
+            total = strip(kind, sides[1 - h], h) + decode(
+                in_a.at[kind, h, 0], insize_a.at[kind, h, 0]
+            )
+            encode(total, code_b.at[kind, h], size_b.at[kind, h])
+            hop_b_size[kind, h].start()
+            hop_b[kind, h].start()
+
+    def stage_three(kind):
+        for h in range(2):
+            hop_a[kind, h, 1].wait_recv()
+            hop_b_size[kind, h].wait_recv()
+            hop_b[kind, h].wait_recv()
+            total = strip(kind, col, h)
+            total = total + decode(in_a.at[kind, h, 1], insize_a.at[kind, h, 1])
+            total = total + decode(in_b.at[kind, h], insize_b.at[kind, h])
+            for place, j in enumerate(halves[h]):
+                part = total[place * shard : (place + 1) * shard]
+                if j > 0:
+                    encode(part, code_z.at[kind, j - 1], size_z.at[kind, j - 1])
+                    hop_z_size[kind, j].start()
+                    hop_z[kind, j].start()
+                else:
+                    grads[kind, col, z] = part
+
+    def finish(kind):
+        total = grads[kind, col, z]
+        for j in far:
+            hop_z_size[kind, j].wait_recv()
+            hop_z[kind, j].wait_recv()
+            total = total + decode(in_z.at[kind, j - 1], insize_z.at[kind, j - 1])
+        out_ref[0, :, kind * channels : (kind + 1) * channels] = total
 
     def weight_grad(section, kind):
-        if kind == 0:
-            term = contract_rows(normed[section], gradpre[section])
-        else:
-            term = contract_rows(acts[section], cots[section])
+        left, right = (normed, gradpre) if kind == 0 else (acts, cots)
+        term = contract_rows(
+            left[section].reshape(2 * total_rows, channels),
+            right[section].reshape(2 * total_rows, channels),
+        )
         for owner in range(dp):
-            grads[section, kind, owner % 4, owner // 4] = term[
-                owner * shard : (owner + 1) * shard
-            ]
+            grads[kind, owner % 4, owner // 4] = term[owner * shard : (owner + 1) * shard]
 
     def grad_preact(section):
         def body(g, carry):
             span = pl.ds(pl.multiple_of(g * joint * rows, rows), joint * rows)
-            product = contract_cols(cots[section, span, :], weights[section, 1])
-            gradpre[section, span, :] = (product * slopes[section, span, :]).astype(jnp.bfloat16)
+            product = contract_cols(cots[section, 0, span, :], weights[section, 1])
+            gradpre[section, 0, span, :] = (product * slopes[section, span, :]).astype(
+                jnp.bfloat16
+            )
             return carry
 
-        lax.fori_loop(0, images // joint, body, 0)
+        lax.fori_loop(0, groups, body, 0)
 
     def grad_normed(section):
         gain_row = pbuf[section, 0]
 
         def body(g, carry):
             span = pl.ds(pl.multiple_of(g * joint * rows, rows), joint * rows)
-            product = contract_cols(gradpre[section, span, :], weights[section, 0])
+            product = contract_cols(gradpre[section, 0, span, :], weights[section, 0])
             for j in range(joint):
                 i = g * joint + j
                 where = pl.ds(pl.multiple_of(i * rows, rows), rows)
@@ -711,55 +747,56 @@
                 )
             return carry
 
-        lax.fori_loop(0, images // joint, body, 0)
-
+        lax.fori_loop(0, groups, body, 0)
+
+    def only(which):
+        return pl.when(core == which)
+
+    only(0)(share["cots"].start)
     grad_preact(1)
-    weight_grad(1, 1)
-    weight_grad(1, 0)
-    swap(1)
+    only(0)(share["gradpre"].start)
+
+    @only(1)
+    def _():
+        share["acts"].wait_recv()
+        share["cots"].wait_recv()
+        weight_grad(1, 1)
+        stage_one(1)
+        share["normed"].wait_recv()
+        share["gradpre"].wait_recv()
+        weight_grad(1, 0)
+        stage_one(0)
+
     grad_normed(1)
-    turn_of(0)
+
+    @only(1)
+    def _():
+        stage_two(1)
+
     pull_back(1, 1)
-    turn_of(1)
+    only(1)(share["cots"].start)
     grad_preact(0)
-    turn_of(2)
-    weight_grad(0, 1)
-    turn_of(3)
-    weight_grad(0, 0)
-    swap(0)
-    for turn in range(4, len(pieces) + LEAD + 1):
-        turn_of(turn)
-    for section in (1, 0):
-        total = mine(section, col, 0)[...]
-        for dz in chunks[:-1]:
-            last[section, dz].wait_recv()
-            total = total + inbox3[section, dz]
-        result[section] = total
-    closing = remote(result.at[other], closed, partner)
-    closing.wait_recv()
-    ours, theirs = result[core], closed[...]
-    out_ref[0, :, :channels] = jnp.where(core == 0, ours, theirs)
-    out_ref[0, :, channels:] = jnp.where(core == 0, theirs, ours)
-    for copy in pending:
+    only(1)(share["gradpre"].start)
+
+    @only(0)
+    def _():
+        share["acts"].wait_recv()
+        share["cots"].wait_recv()
+        weight_grad(0, 1)
+        stage_one(1)
+        share["normed"].wait_recv()
+        share["gradpre"].wait_recv()
+        weight_grad(0, 0)
+        stage_one(0)
+        stage_two(1)
+
+    stage_three(1)
+    stage_two(0)
+    stage_three(0)
+    finish(1)
+    finish(0)
+    for copy in sent:
         copy.wait_send()
-    for way in (1, -1):
-
-        @pl.when(goes_on(way))
-        def _(way=way):
-            line[way, 0].wait_send()
-
-    for way, hop in slots:
-
-        @pl.when(holds(way, hop))
-        def _(way=way, hop=hop):
-            sent = [spread_x[way, hop], spread_y[way, hop]] + diag[way, hop]
-            for copy in sent + core_sends[way, hop]:
-                copy.wait_send()
-            if hop + 1 < depth - 1:
-
-                @pl.when(goes_on(way))
-                def _():
-                    line[way, hop + 1].wait_send()
 
 
 def fused_body(latents, noise, timesteps, reward_dir, gain, time_scale, w_in, w_out):
@@ -773,11 +810,21 @@
     loss_scale = 1.0 / math.sqrt(dp * latents.shape[0])
     shape = (dp, depth, shard, channels, images, rows, loss_scale)
     total_rows = images * rows
-    bf16, f32 = jnp.bfloat16, jnp.float32
+    strip_rows = depth // 2 * shard
+    bf16, f32, i16 = jnp.bfloat16, jnp.float32, jnp.int16
     lines = -(-2 * images // 8) * 8
     square = (shard, channels)
-    copies = 64 * depth
+    line = (1, channels)
+    copies = 14 * depth + 26
     vmem = pl.BlockSpec(memory_space=pltpu.VMEM)
+    codes = [
+        pltpu.VMEM((2, 2, 2, strip_rows, channels), i16),
+        pltpu.VMEM((2, 2, strip_rows, channels), i16),
+        pltpu.VMEM((2, depth - 1) + square, i16),
+        pltpu.VMEM((2, 2, 2) + line, f32),
+        pltpu.VMEM((2, 2) + line, f32),
+        pltpu.VMEM((2, depth - 1) + line, f32),
+    ]
     grad_rows = pl.pallas_call(
         functools.partial(step_kernel, shape),
         out_shape=jax.ShapeDtypeStruct((1, shard, 2 * channels), f32),
@@ -787,29 +834,27 @@
         scratch_shapes=[
             pltpu.VMEM((-(-images // 8) * 8, channels), f32),
             pltpu.VMEM((3, -(-images // 8) * 8, 128), f32),
-            pltpu.VMEM((2, 4, depth, 2) + square, bf16),
+            pltpu.VMEM((2, 2, 4, depth) + square, bf16),
             pltpu.VMEM((2, 2, 1, channels), f32),
             pltpu.VMEM((2, 2, channels, channels), bf16),
             pltpu.VMEM((3, total_rows, channels), bf16),
             pltpu.VMEM((total_rows, channels), bf16),
-            pltpu.VMEM((2, total_rows, channels), bf16),
+            pltpu.VMEM((2, 2, total_rows, channels), bf16),
             pltpu.VMEM((2, total_rows, channels), f32),
-            pltpu.VMEM((2, total_rows, channels), bf16),
-            pltpu.VMEM((2, total_rows, channels), bf16),
-            pltpu.VMEM((2, total_rows, channels), bf16),
+            pltpu.VMEM((2, 2, total_rows, channels), bf16),
+            pltpu.VMEM((2, 2, total_rows, channels), bf16),
+            pltpu.VMEM((2, 2, total_rows, channels), bf16),
             pltpu.VMEM((3, lines, channels), f32),
             pltpu.VMEM((3, lines, channels), f32),
             pltpu.VMEM((lines, channels), f32),
             pltpu.VMEM((total_rows, channels), f32),
             pltpu.VMEM((channels, 128), bf16),
             pltpu.VMEM((128, channels), bf16),
-            pltpu.VMEM((2, 2, 4, depth) + square, f32),
             pltpu.VMEM((2, 4, depth) + square, f32),
-            pltpu.VMEM((2, 2, depth) + square, f32),
-            pltpu.VMEM((2, depth) + square, f32),
-            pltpu.VMEM((2, depth) + square, f32),
-            pltpu.VMEM((2,) + square, f32),
-            pltpu.VMEM(square, f32),
+        ]
+        + codes
+        + codes
+        + [
             pltpu.SemaphoreType.DMA((copies,)),
             pltpu.SemaphoreType.DMA((copies,)),
             pltpu.SemaphoreType.DMA((6,)),
@@ -822,7 +867,8 @@
 
 
 def fits(mesh):
-    return mesh.shape["segment"] == 2 and mesh.shape["dp"] % 4 == 0 and mesh.shape["dp"] >= 16
+    dp = mesh.shape["dp"]
+    return mesh.shape["segment"] == 2 and dp >= 16 and dp & (dp - 1) == 0
 
 
 def solution(mesh):

time: 78.8 us -> 67 us (0.85)
  Pallas kernels: 77 us -> 65.1 us
    pallas_call x1, Pallas kernels: 77 us -> 65.1 us  [fused_body(): pl.pallas_call(functools.partial(step_kernel, shape), out_shape=jax.Shape...]
where the time goes in v1:
time: 67 us; the launch traced here: 66.8 us
  Pallas kernels  65.1 us (97%)
  local copies, waits for them, and re-layouts  1.62 us (2%)
    pallas_call x1, Pallas kernels, fused_body(): pl.pallas_call(functools.partial(step_kernel, shape), out_shape=jax.Shape...  65.1 us
    unnamed x1, local copies, waits for them, and re-layouts  1.62 us

profile of v1, /device:TPU:0, one launch (start us, length us, event | category | flops | bytes accessed | tf_op | source)
XLA Modules:
  0.0 66.8 jit_solution(9864039734520714854)
XLA Ops:
  0.0 65.1 %shard_map.82 = f32[1,40,1280]{2,1,0:T(8,128)} custom-call(bf16[1,40,640]{2,1,0:T(8,128)(2,1)} %win_ref.1, bf16[1,40,640]{2,1,0:T(8,128)(2,1)} %wout_ref.1, f32[1,640]{1,0:T(1,128)} %gain_ref.1, f32[1,640]{1,0:T(1,128)} %time_ref.1, bf16[1024,640]{1,0:T(8,128)(2,1)} %latent_ref.1, bf16[1024,640]{1,0:T(8,128)(2,1)} %noise_ref.1, s32[8]{0:T(128)} %times_ref.1, ...), custom_call_target="tpu_custom_call" | custom-call | tf_op jit(solution)/shard_map/pallas_call | solution.py:828
  65.2 1.6 %copy.10 = f32[1,40,1280]{2,1,0:T(8,128)} copy(f32[1,40,1280]{2,1,0:T(8,128)} %shard_map.82) | data formatting | bytes 409600

commit v2 on v1

--- a/solution.py
+++ b/solution.py
@@ -11,6 +11,7 @@
 GROUPS = 32
 NSTEPS = 1000
 STRIDE = 20
+LINE = 4
 LIMIT = 32760.0
 TINY = 1e-30
 
@@ -259,11 +260,9 @@
     weights,
     states,
     noises,
-    normed,
+    lefts,
     slopes,
-    acts,
-    cots,
-    gradpre,
+    rights,
     means,
     scales,
     sums,
@@ -271,6 +270,9 @@
     gather_mat,
     scatter_mat,
     grads,
+    kept,
+    given,
+    gift,
     code_a,
     code_b,
     code_z,
@@ -299,6 +301,9 @@
     qd = 3 - col
     x_dev = (z * 4 + qx, core)
     y_dev = (z * 4 + qy, core)
+    qu = qx + core * (qy - qx)
+    qv = qy + core * (qx - qy)
+    u_dev, v_dev = (z * 4 + qu, core), (z * 4 + qv, core)
     partner = (me, other)
 
     def flipped(j):
@@ -315,17 +320,22 @@
     far = list(range(1, depth))
     early = list(range(depth // 2))
     late = list(range(depth // 2, depth))
-    count = [0]
+    outgoing, incoming_slots = [0], [0]
     sent = []
 
-    def reserve(src, dst, device):
-        k = count[0]
-        count[0] += 1
+    def slots(number):
+        first = incoming_slots[0]
+        incoming_slots[0] += number
+        return first
+
+    def reserve(src, dst, device, slot=None):
+        k = outgoing[0]
+        outgoing[0] += 1
         copy = pltpu.make_async_remote_copy(
             src_ref=src,
             dst_ref=dst,
             send_sem=send_sem.at[k],
-            recv_sem=recv_sem.at[k],
+            recv_sem=recv_sem.at[slots(1) if slot is None else slot],
             device_id=device,
             device_id_type=pl.DeviceIdType.MESH,
         )
@@ -379,26 +389,31 @@
         reserve(gain_ref, pbuf.at[core, 0], partner),
         reserve(time_ref, pbuf.at[core, 1], partner),
     ]
-    to_x, to_y, to_z, to_core, to_diag, blocks = {}, {}, {}, {}, {}, {}
+    to_u, to_v, to_z, to_core, to_diag, blocks = {}, {}, {}, {}, {}, {}
     for section in range(2):
+        own = piece(section, col, 0)
         for j in range(depth):
             here = piece(section, col, j)
-            to_x[section, j] = reserve(here, here, x_dev)
-            to_y[section, j] = reserve(here, here, y_dev)
+            to_u[section, j] = reserve(here, here, u_dev)
+            to_v[section, j] = reserve(here, here, v_dev)
             if j > 0:
                 to_core[section, j] = reserve(here, here, partner)
-                own = piece(section, col, 0)
                 to_z[section, j] = reserve(own, own, z_dev[j])
-            q, device = (qx, y_dev) if j in early else (qy, x_dev)
+            q, device = (qu, v_dev) if j in early else (qv, u_dev)
             passed = piece(section, q, j)
             to_diag[section, j] = reserve(passed, passed, device)
-        for q, name in ((qx, "x"), (qy, "y"), (qd, "d")):
+        for q, name in ((qu, "u"), (qv, "v"), (qd, "d")):
             whole = wbuf.at[section, core, q]
             blocks[section, name] = reserve(whole, whole, partner)
 
-    def send_own(section):
-        to_x[section, 0].start()
-        to_y[section, 0].start()
+    def only(which):
+        return pl.when(core == which)
+
+    def own_sides(section):
+        to_u[section, 0].start()
+        to_v[section, 0].start()
+
+    def own_line(section):
         for j in far:
             to_z[section, j].start()
 
@@ -408,41 +423,43 @@
 
     for copy in swap:
         copy.start()
-    for mine in range(2):
-
-        @pl.when(core == mine)
-        def _(mine=mine):
-            send_own(mine)
-
-    take_swap()
-    for mine in range(2):
-
-        @pl.when(core == mine)
-        def _(mine=mine):
-            send_own(1 - mine)
+
+    @only(0)
+    def _():
+        own_sides(0)
+        own_line(0)
+        take_swap()
+        own_sides(1)
+        own_line(1)
+
+    @only(1)
+    def _():
+        own_sides(1)
+        take_swap()
+        own_line(0)
+        own_sides(0)
+        own_line(1)
 
     for copy in tunes:
         copy.start()
 
-    def pass_line(section, steps):
-        for j in steps:
-            to_z[section, j].wait_recv()
-            to_x[section, j].start()
-            to_y[section, j].start()
-            to_core[section, j].start()
-
-    def pass_diag(section, steps):
-        for j in steps:
-            (to_x if j in early else to_y)[section, j].wait_recv()
-            to_diag[section, j].start()
+    def pass_line(section, j):
+        to_z[section, j].wait_recv()
+        to_u[section, j].start()
+        to_v[section, j].start()
+        to_core[section, j].start()
+
+    def pass_diag(section, j):
+        (to_u if j in early else to_v)[section, j].wait_recv()
+        to_diag[section, j].start()
 
     def pass_sides(section):
         for j in late:
-            to_x[section, j].wait_recv()
-        blocks[section, "x"].start()
+            to_u[section, j].wait_recv()
+        blocks[section, "u"].start()
         for j in early:
-            to_y[section, j].wait_recv()
-        blocks[section, "y"].start()
+            to_v[section, j].wait_recv()
+        blocks[section, "v"].start()
 
     def pass_corner(section):
         for j in range(depth):
@@ -452,7 +469,7 @@
     def arrived(section):
         for j in far:
             to_core[section, j].wait_recv()
-        for name in ("x", "y", "d"):
+        for name in ("u", "v", "d"):
             blocks[section, name].wait_recv()
 
     def column(stacked):
@@ -464,18 +481,19 @@
             )
         return values
 
-    half_width = channels // 2
-    lane = lax.broadcasted_iota(jnp.int32, embed_ref.shape, 1)
-    k_index = jnp.where(lane < half_width, lane, lane - half_width).astype(jnp.float32)
-    phases = column(embed_ref) * jnp.exp(-math.log(10000.0) * k_index / half_width)
-    embed_ref[...] = jnp.where(lane < half_width, jnp.sin(phases), jnp.cos(phases))
-    now = column(coef_ref.at[0])
-    ab_now, ab_prev = alpha_bar(now), alpha_bar(now - STRIDE)
-    coef_a, coef_b = jnp.sqrt(ab_now), jnp.sqrt(1.0 - ab_now)
-    coef_p, coef_q = jnp.sqrt(ab_prev), jnp.sqrt(0.75 * (1.0 - ab_prev))
-    coef_ref[0] = coef_p / coef_a
-    coef_ref[1] = coef_q - coef_p * coef_b / coef_a
-    coef_ref[2] = 0.5 * jnp.sqrt(1.0 - ab_prev)
+    def embed_all():
+        half_width = channels // 2
+        lane = lax.broadcasted_iota(jnp.int32, embed_ref.shape, 1)
+        k_index = jnp.where(lane < half_width, lane, lane - half_width).astype(jnp.float32)
+        phases = column(embed_ref) * jnp.exp(-math.log(10000.0) * k_index / half_width)
+        embed_ref[...] = jnp.where(lane < half_width, jnp.sin(phases), jnp.cos(phases))
+        now = column(coef_ref.at[0])
+        ab_now, ab_prev = alpha_bar(now), alpha_bar(now - STRIDE)
+        coef_a, coef_b = jnp.sqrt(ab_now), jnp.sqrt(1.0 - ab_now)
+        coef_p, coef_q = jnp.sqrt(ab_prev), jnp.sqrt(0.75 * (1.0 - ab_prev))
+        coef_ref[0] = coef_p / coef_a
+        coef_ref[1] = coef_q - coef_p * coef_b / coef_a
+        coef_ref[2] = 0.5 * jnp.sqrt(1.0 - ab_prev)
 
     def group_means(values):
         parts = jnp.dot(
@@ -517,7 +535,7 @@
 
         def norm_body(i, carry):
             where = pl.ds(pl.multiple_of(i * rows, rows), rows)
-            normed[section, 0, where, :] = (unit(section, i) * gain_row).astype(jnp.bfloat16)
+            lefts[0, section, 0, where, :] = (unit(section, i) * gain_row).astype(jnp.bfloat16)
             return carry
 
         lax.fori_loop(0, images, norm_body, 0)
@@ -546,7 +564,7 @@
         def forward_body(g, carry):
             span = pl.ds(pl.multiple_of(g * joint * rows, rows), joint * rows)
             product = jnp.dot(
-                normed[section, 0, span, :],
+                lefts[0, section, 0, span, :],
                 weights[section, 0],
                 preferred_element_type=jnp.float32,
             )
@@ -555,10 +573,10 @@
                 where = pl.ds(pl.multiple_of(i * rows, rows), rows)
                 preact = product[j * rows : (j + 1) * rows] + time_row * embed_ref[pl.ds(i, 1), :]
                 gate = jax.nn.sigmoid(preact)
-                acts[section, 0, where, :] = (preact * gate).astype(jnp.bfloat16)
+                lefts[1, section, 0, where, :] = (preact * gate).astype(jnp.bfloat16)
                 slopes[section, where, :] = gate * (1.0 + preact * (1.0 - gate))
             product = jnp.dot(
-                acts[section, 0, span, :],
+                lefts[1, section, 0, span, :],
                 weights[section, 1],
                 preferred_element_type=jnp.float32,
             )
@@ -569,39 +587,48 @@
 
         lax.fori_loop(start, stop, forward_body, 0)
 
-    pass_line(0, far[:1])
+    share_left = [
+        reserve(lefts.at[other, section, 0], lefts.at[other, section, 1], partner)
+        for section in range(2)
+    ]
+    share_right = [
+        reserve(rights.at[other, section, 0], rights.at[other, section, 1], partner)
+        for section in range(2)
+    ]
+    pass_line(0, 1)
+    pass_diag(0, 0)
+    pass_line(0, 2)
+    pass_line(0, 3)
+    pass_diag(0, 1)
+    pass_line(1, 1)
     for copy in tunes:
         copy.wait_recv()
     for copy in locals_[4:]:
         copy.wait()
-    pass_diag(0, early[:1])
-    pass_line(0, far[1:])
-    pass_diag(0, early[1:])
-    pass_line(1, far[:1])
     normalize(0)
-    pass_diag(0, late)
-    pass_line(1, far[1:])
+    embed_all()
+    pass_diag(0, 2)
+    pass_diag(0, 3)
+    pass_line(1, 2)
+    pass_line(1, 3)
     pass_sides(0)
     pass_corner(0)
-    pass_diag(1, early)
+    pass_diag(1, 0)
+    pass_diag(1, 1)
     arrived(0)
     lay_out(0)
     forward(0, 0, groups // 2)
-    pass_diag(1, late)
+    pass_diag(1, 2)
+    pass_diag(1, 3)
     pass_sides(1)
     forward(0, groups // 2, groups)
+    share_left[0].start()
     pass_corner(1)
     normalize(1)
     arrived(1)
     lay_out(1)
     forward(1, 0, groups)
-
-    share = {
-        name: reserve(ref.at[other, 0], ref.at[other, 1], partner)
-        for name, ref in (("normed", normed), ("acts", acts), ("cots", cots), ("gradpre", gradpre))
-    }
-    share["acts"].start()
-    share["normed"].start()
+    share_left[1].start()
 
     statistics(2)
 
@@ -632,8 +659,8 @@
                 - unit(stage, i) * sums[pl.ds(images + i, 1), :]
             )
             if incoming is not None:
-                pulled = cots[incoming, 0, where, :].astype(jnp.float32) + pulled
-            cots[stage - 1, 0, where, :] = pulled.astype(jnp.bfloat16)
+                pulled = rights[1, incoming, 0, where, :].astype(jnp.float32) + pulled
+            rights[1, stage - 1, 0, where, :] = pulled.astype(jnp.bfloat16)
             return carry
 
         lax.fori_loop(0, images, body, 0)
@@ -644,86 +671,118 @@
     sides = (qx, qy)
     side_devs = (x_dev, y_dev)
     hop_a, hop_a_size, hop_b, hop_b_size, hop_z, hop_z_size = {}, {}, {}, {}, {}, {}
-    for kind in (1, 0):
+    z_slots = slots(4 * len(far))
+    for section in (1, 0):
         for h in range(2):
             for step in range(2):
-                hop_a[kind, h, step] = reserve(
-                    code_a.at[kind, h, step], in_a.at[kind, h, step], side_devs[h]
+                hop_a[section, h, step] = reserve(
+                    code_a.at[section, h, step], in_a.at[section, h, step], side_devs[h]
                 )
-            hop_a_size[kind, h] = reserve(
-                size_a.at[kind, h], insize_a.at[kind, h], side_devs[h]
-            )
-            hop_b[kind, h] = reserve(code_b.at[kind, h], in_b.at[kind, h], side_devs[1 - h])
-            hop_b_size[kind, h] = reserve(
-                size_b.at[kind, h], insize_b.at[kind, h], side_devs[1 - h]
+            hop_a_size[section, h] = reserve(
+                size_a.at[section, h], insize_a.at[section, h], side_devs[h]
+            )
+            hop_b[section, h] = reserve(
+                code_b.at[section, h], in_b.at[section, h], side_devs[1 - h]
+            )
+            hop_b_size[section, h] = reserve(
+                size_b.at[section, h], insize_b.at[section, h], side_devs[1 - h]
             )
         for j in far:
-            hop_z[kind, j] = reserve(code_z.at[kind, j - 1], in_z.at[kind, j - 1], z_dev[j])
-            hop_z_size[kind, j] = reserve(
-                size_z.at[kind, j - 1], insize_z.at[kind, j - 1], z_dev[j]
-            )
-
-    def strip(kind, q, h):
-        return jnp.concatenate([grads[kind, q, zj[j]] for j in halves[h]], axis=0)
-
-    def stage_one(kind):
+            slot = z_slots + core * (2 * len(far)) + 2 * (j - 1)
+            device = (zj[j] * 4 + col, section)
+            hop_z[section, j] = reserve(
+                code_z.at[section, j - 1], in_z.at[core, j - 1], device, slot
+            )
+            hop_z_size[section, j] = reserve(
+                size_z.at[section, j - 1], insize_z.at[core, j - 1], device, slot + 1
+            )
+    hand_over = reserve(given, gift, partner)
+
+    def strip(section, q, h):
+        return jnp.concatenate([grads[section, q, zj[j]] for j in halves[h]], axis=0)
+
+    def stage_one(section):
         for h in range(2):
             for step, q in enumerate((qd, sides[h])):
-                encode(strip(kind, q, h), code_a.at[kind, h, step], size_a.at[kind, h, step])
-            hop_a_size[kind, h].start()
+                encode(
+                    strip(section, q, h),
+                    code_a.at[section, h, step],
+                    size_a.at[section, h, step],
+                )
+            hop_a_size[section, h].start()
             for step in range(2):
-                hop_a[kind, h, step].start()
-
-    def stage_two(kind):
+                hop_a[section, h, step].start()
+
+    def stage_two(section):
         for h in range(2):
-            hop_a_size[kind, h].wait_recv()
-            hop_a[kind, h, 0].wait_recv()
-            total = strip(kind, sides[1 - h], h) + decode(
-                in_a.at[kind, h, 0], insize_a.at[kind, h, 0]
-            )
-            encode(total, code_b.at[kind, h], size_b.at[kind, h])
-            hop_b_size[kind, h].start()
-            hop_b[kind, h].start()
-
-    def stage_three(kind):
+            hop_a_size[section, h].wait_recv()
+            hop_a[section, h, 0].wait_recv()
+            total = strip(section, sides[1 - h], h) + decode(
+                in_a.at[section, h, 0], insize_a.at[section, h, 0]
+            )
+            encode(total, code_b.at[section, h], size_b.at[section, h])
+            hop_b_size[section, h].start()
+            hop_b[section, h].start()
+
+    def stage_three(section):
         for h in range(2):
-            hop_a[kind, h, 1].wait_recv()
-            hop_b_size[kind, h].wait_recv()
-            hop_b[kind, h].wait_recv()
-            total = strip(kind, col, h)
-            total = total + decode(in_a.at[kind, h, 1], insize_a.at[kind, h, 1])
-            total = total + decode(in_b.at[kind, h], insize_b.at[kind, h])
+            hop_a[section, h, 1].wait_recv()
+            hop_b_size[section, h].wait_recv()
+            hop_b[section, h].wait_recv()
+            total = strip(section, col, h)
+            total = total + decode(in_a.at[section, h, 1], insize_a.at[section, h, 1])
+            total = total + decode(in_b.at[section, h], insize_b.at[section, h])
             for place, j in enumerate(halves[h]):
                 part = total[place * shard : (place + 1) * shard]
                 if j > 0:
-                    encode(part, code_z.at[kind, j - 1], size_z.at[kind, j - 1])
-                    hop_z_size[kind, j].start()
-                    hop_z[kind, j].start()
+                    encode(part, code_z.at[section, j - 1], size_z.at[section, j - 1])
+                    hop_z_size[section, j].start()
+                    hop_z[section, j].start()
                 else:
-                    grads[kind, col, z] = part
-
-    def finish(kind):
-        total = grads[kind, col, z]
-        for j in far:
-            hop_z_size[kind, j].wait_recv()
-            hop_z[kind, j].wait_recv()
-            total = total + decode(in_z.at[kind, j - 1], insize_z.at[kind, j - 1])
-        out_ref[0, :, kind * channels : (kind + 1) * channels] = total
-
-    def weight_grad(section, kind):
-        left, right = (normed, gradpre) if kind == 0 else (acts, cots)
+
+                    @only(section)
+                    def _(part=part):
+                        kept[...] = part
+
+                    @only(1 - section)
+                    def _(part=part):
+                        given[...] = part
+                        hand_over.start()
+
+    def finish():
+        hand_over.wait_recv()
+        for kind in range(2):
+            total = jnp.where(core == kind, kept[...], gift[...])
+            for j in far:
+                slot = z_slots + kind * (2 * len(far)) + 2 * (j - 1)
+                for source, target, k in (
+                    (size_z, insize_z, slot + 1),
+                    (code_z, in_z, slot),
+                ):
+                    pltpu.make_async_remote_copy(
+                        src_ref=source.at[0, j - 1],
+                        dst_ref=target.at[kind, j - 1],
+                        send_sem=send_sem.at[0],
+                        recv_sem=recv_sem.at[k],
+                        device_id=z_dev[j],
+                        device_id_type=pl.DeviceIdType.MESH,
+                    ).wait_recv()
+                total = total + decode(in_z.at[kind, j - 1], insize_z.at[kind, j - 1])
+            out_ref[0, :, kind * channels : (kind + 1) * channels] = total
+
+    def weight_grad(section):
         term = contract_rows(
-            left[section].reshape(2 * total_rows, channels),
-            right[section].reshape(2 * total_rows, channels),
+            lefts[core, section].reshape(2 * total_rows, channels),
+            rights[core, section].reshape(2 * total_rows, channels),
         )
         for owner in range(dp):
-            grads[kind, owner % 4, owner // 4] = term[owner * shard : (owner + 1) * shard]
+            grads[section, owner % 4, owner // 4] = term[owner * shard : (owner + 1) * shard]
 
     def grad_preact(section):
         def body(g, carry):
             span = pl.ds(pl.multiple_of(g * joint * rows, rows), joint * rows)
-            product = contract_cols(cots[section, 0, span, :], weights[section, 1])
-            gradpre[section, 0, span, :] = (product * slopes[section, span, :]).astype(
+            product = contract_cols(rights[1, section, 0, span, :], weights[section, 1])
+            rights[0, section, 0, span, :] = (product * slopes[section, span, :]).astype(
                 jnp.bfloat16
             )
             return carry
@@ -735,7 +794,7 @@
 
         def body(g, carry):
             span = pl.ds(pl.multiple_of(g * joint * rows, rows), joint * rows)
-            product = contract_cols(gradpre[section, 0, span, :], weights[section, 0])
+            product = contract_cols(rights[0, section, 0, span, :], weights[section, 0])
             for j in range(joint):
                 i = g * joint + j
                 where = pl.ds(pl.multiple_of(i * rows, rows), rows)
@@ -749,52 +808,27 @@
 
         lax.fori_loop(0, groups, body, 0)
 
-    def only(which):
-        return pl.when(core == which)
-
-    only(0)(share["cots"].start)
+    only(0)(share_right[1].start)
     grad_preact(1)
-    only(0)(share["gradpre"].start)
-
-    @only(1)
-    def _():
-        share["acts"].wait_recv()
-        share["cots"].wait_recv()
-        weight_grad(1, 1)
-        stage_one(1)
-        share["normed"].wait_recv()
-        share["gradpre"].wait_recv()
-        weight_grad(1, 0)
-        stage_one(0)
-
+    only(1)(share_right[1].start)
     grad_normed(1)
-
-    @only(1)
-    def _():
-        stage_two(1)
-
+    share_left[1].wait_recv()
+    share_right[1].wait_recv()
+    weight_grad(1)
+    stage_one(1)
     pull_back(1, 1)
-    only(1)(share["cots"].start)
+    only(0)(share_right[0].start)
     grad_preact(0)
-    only(1)(share["gradpre"].start)
-
-    @only(0)
-    def _():
-        share["acts"].wait_recv()
-        share["cots"].wait_recv()
-        weight_grad(0, 1)
-        stage_one(1)
-        share["normed"].wait_recv()
-        share["gradpre"].wait_recv()
-        weight_grad(0, 0)
-        stage_one(0)
-        stage_two(1)
-
+    only(1)(share_right[0].start)
+    stage_two(1)
+    share_left[0].wait_recv()
+    share_right[0].wait_recv()
+    weight_grad(0)
+    stage_one(0)
     stage_three(1)
     stage_two(0)
     stage_three(0)
-    finish(1)
-    finish(0)
+    finish()
     for copy in sent:
         copy.wait_send()
 
@@ -815,7 +849,8 @@
     lines = -(-2 * images // 8) * 8
     square = (shard, channels)
     line = (1, channels)
-    copies = 14 * depth + 26
+    far = depth - 1
+    copies = 2 * (3 * depth + 2 * far + 3) + 4 * far + 29
     vmem = pl.BlockSpec(memory_space=pltpu.VMEM)
     codes = [
         pltpu.VMEM((2, 2, 2, strip_rows, channels), i16),
@@ -839,11 +874,9 @@
             pltpu.VMEM((2, 2, channels, channels), bf16),
             pltpu.VMEM((3, total_rows, channels), bf16),
             pltpu.VMEM((total_rows, channels), bf16),
-            pltpu.VMEM((2, 2, total_rows, channels), bf16),
+            pltpu.VMEM((2, 2, 2, total_rows, channels), bf16),
             pltpu.VMEM((2, total_rows, channels), f32),
-            pltpu.VMEM((2, 2, total_rows, channels), bf16),
-            pltpu.VMEM((2, 2, total_rows, channels), bf16),
-            pltpu.VMEM((2, 2, total_rows, channels), bf16),
+            pltpu.VMEM((2, 2, 2, total_rows, channels), bf16),
             pltpu.VMEM((3, lines, channels), f32),
             pltpu.VMEM((3, lines, channels), f32),
             pltpu.VMEM((lines, channels), f32),
@@ -851,6 +884,9 @@
             pltpu.VMEM((channels, 128), bf16),
             pltpu.VMEM((128, channels), bf16),
             pltpu.VMEM((2, 4, depth) + square, f32),
+            pltpu.VMEM(square, f32),
+            pltpu.VMEM(square, f32),
+            pltpu.VMEM(square, f32),
         ]
         + codes
         + codes
@@ -867,8 +903,7 @@
 
 
 def fits(mesh):
-    dp = mesh.shape["dp"]
-    return mesh.shape["segment"] == 2 and dp >= 16 and dp & (dp - 1) == 0
+    return mesh.shape["segment"] == 2 and mesh.shape["dp"] == 4 * LINE
 
 
 def solution(mesh):

time: 67 us -> 60.1 us (0.90)
  Pallas kernels: 65.1 us -> 58.3 us
    pallas_call x1, Pallas kernels: 65.1 us -> 58.3 us  [fused_body(): pl.pallas_call(functools.partial(step_kernel, shape), out_shape=jax.Shape...]
where the time goes in v2:
time: 60.1 us; the launch traced here: 59.9 us
  Pallas kernels  58.3 us (97%)
  local copies, waits for them, and re-layouts  1.62 us (3%)
    pallas_call x1, Pallas kernels, fused_body(): pl.pallas_call(functools.partial(step_kernel, shape), out_shape=jax.Shape...  58.3 us
    unnamed x1, local copies, waits for them, and re-layouts  1.62 us

profile of v2, /device:TPU:0, one launch (start us, length us, event | category | flops | bytes accessed | tf_op | source)
XLA Modules:
  0.0 59.9 jit_solution(4452109478546303855)
XLA Ops:
  0.0 58.3 %shard_map.82 = f32[1,40,1280]{2,1,0:T(8,128)} custom-call(bf16[1,40,640]{2,1,0:T(8,128)(2,1)} %win_ref.1, bf16[1,40,640]{2,1,0:T(8,128)(2,1)} %wout_ref.1, f32[1,640]{1,0:T(1,128)} %gain_ref.1, f32[1,640]{1,0:T(1,128)} %time_ref.1, bf16[1024,640]{1,0:T(8,128)(2,1)} %latent_ref.1, bf16[1024,640]{1,0:T(8,128)(2,1)} %noise_ref.1, s32[8]{0:T(128)} %times_ref.1, ...), custom_call_target="tpu_custom_call" | custom-call | tf_op jit(solution)/shard_map/pallas_call | solution.py:863
  58.3 1.6 %copy.10 = f32[1,40,1280]{2,1,0:T(8,128)} copy(f32[1,40,1280]{2,1,0:T(8,128)} %shard_map.82) | data formatting | bytes 409600

commit v3 on v2

--- a/solution.py
+++ b/solution.py
@@ -250,9 +250,11 @@
     time_ref,
     latent_ref,
     noise_ref,
+    times_in,
+    reward_in,
+    out_ref,
     times_ref,
     reward_ref,
-    out_ref,
     embed_ref,
     coef_ref,
     wbuf,
@@ -353,6 +355,8 @@
                 (time_ref, pbuf.at[core, 1]),
                 (latent_ref.at[pl.ds(base, total_rows)], states.at[0]),
                 (noise_ref.at[pl.ds(base, total_rows)], noises),
+                (times_in, times_ref),
+                (reward_in, reward_ref),
             )
         )
     ]
@@ -386,8 +390,8 @@
         for kind in (0, 1)
     ]
     tunes = [
-        reserve(gain_ref, pbuf.at[core, 0], partner),
-        reserve(time_ref, pbuf.at[core, 1], partner),
+        reserve(pbuf.at[core, 0], pbuf.at[core, 0], partner),
+        reserve(pbuf.at[core, 1], pbuf.at[core, 1], partner),
     ]
     to_u, to_v, to_z, to_core, to_diag, blocks = {}, {}, {}, {}, {}, {}
     for section in range(2):
@@ -555,7 +559,7 @@
                     both.astype(jnp.bfloat16)
                 )
 
-    joint = 2 if images % 2 == 0 else 1
+    joint = next(n for n in (4, 2, 1) if images % n == 0)
     groups = images // joint
 
     def forward(section, start, stop):
@@ -587,6 +591,8 @@
 
         lax.fori_loop(start, stop, forward_body, 0)
 
+    gathers = list(sent)
+    del sent[:]
     share_left = [
         reserve(lefts.at[other, section, 0], lefts.at[other, section, 1], partner)
         for section in range(2)
@@ -667,6 +673,9 @@
 
     pull_back(2, None)
 
+    for copy in gathers:
+        copy.wait_send()
+    outgoing[0] = 0
     halves = (late[::-1], early[::-1])
     sides = (qx, qy)
     side_devs = (x_dev, y_dev)
@@ -863,10 +872,11 @@
     grad_rows = pl.pallas_call(
         functools.partial(step_kernel, shape),
         out_shape=jax.ShapeDtypeStruct((1, shard, 2 * channels), f32),
-        in_specs=[vmem] * 4 + [pl.BlockSpec(memory_space=pl.ANY)] * 2
-        + [pl.BlockSpec(memory_space=pltpu.SMEM), vmem],
+        in_specs=[pl.BlockSpec(memory_space=pl.ANY)] * 8,
         out_specs=vmem,
         scratch_shapes=[
+            pltpu.SMEM((micro_count,), jnp.int32),
+            pltpu.VMEM((channels,), f32),
             pltpu.VMEM((-(-images // 8) * 8, channels), f32),
             pltpu.VMEM((3, -(-images // 8) * 8, 128), f32),
             pltpu.VMEM((2, 2, 4, depth) + square, bf16),
@@ -891,9 +901,9 @@
         + codes
         + codes
         + [
+            pltpu.SemaphoreType.DMA((copies - 4 * far - 21,)),
             pltpu.SemaphoreType.DMA((copies,)),
-            pltpu.SemaphoreType.DMA((copies,)),
-            pltpu.SemaphoreType.DMA((6,)),
+            pltpu.SemaphoreType.DMA((8,)),
         ],
         compiler_params=pltpu.CompilerParams(
             collective_id=0, has_side_effects=True, vmem_limit_bytes=60 * 1024 * 1024

time: 60.1 us -> 58 us (0.965)
  Pallas kernels: 58.3 us -> 56.2 us
    pallas_call x1, Pallas kernels: 58.3 us -> 56.2 us  [fused_body(): pl.pallas_call(functools.partial(step_kernel, shape), out_shape=jax.Shape...]
where the time goes in v3:
time: 58 us; the launch traced here: 57.9 us
  Pallas kernels  56.2 us (97%)
  local copies, waits for them, and re-layouts  1.62 us (3%)
    pallas_call x1, Pallas kernels, fused_body(): pl.pallas_call(functools.partial(step_kernel, shape), out_shape=jax.Shape...  56.2 us
    unnamed x1, local copies, waits for them, and re-layouts  1.62 us

profile of v3, /device:TPU:0, one launch (start us, length us, event | category | flops | bytes accessed | tf_op | source)
XLA Modules:
  0.0 57.9 jit_solution(16716155773026311634)
XLA Ops:
  0.0 56.2 %shard_map.82 = f32[1,40,1280]{2,1,0:T(8,128)} custom-call(bf16[1,40,640]{2,1,0:T(8,128)(2,1)} %win_ref.1, bf16[1,40,640]{2,1,0:T(8,128)(2,1)} %wout_ref.1, f32[1,640]{1,0:T(1,128)} %gain_ref.1, f32[1,640]{1,0:T(1,128)} %time_ref.1, bf16[1024,640]{1,0:T(8,128)(2,1)} %latent_ref.1, bf16[1024,640]{1,0:T(8,128)(2,1)} %noise_ref.1, s32[8]{0:T(128)} %times_in.1, ...), custom_call_target="tpu_custom_call" | custom-call | tf_op jit(solution)/shard_map/pallas_call | solution.py:872
  56.2 1.6 %copy.10 = f32[1,40,1280]{2,1,0:T(8,128)} copy(f32[1,40,1280]{2,1,0:T(8,128)} %shard_map.82) | data formatting | bytes 409600
